TPU v7x, 512 devices: a whole 4x4x16 slice. The times are simulated.
512 devices in a mesh: seq: 128 (over x, y_hi, z), fsdp: 4 (over y_lo, core).
Axes of the slice: x: 4, y: 4 (y_hi: 2, y_lo: 2; y = y_hi * 2 + y_lo), z: 16, core: 2. Of those that a mesh axis runs over, the one named last changes fastest.
Arguments:
- block_input: bfloat16 [8, 16384, 1536], P('fsdp', 'seq'), may hold values from -6 to 6
- dilated_weight: bfloat16 [3, 1536, 768], P(None, 'fsdp'), may hold values from -0.09375 to 0.09375
- w_project: bfloat16 [768, 1536], P('fsdp'), may hold values from -0.21875 to 0.21875
- gain_first: float32 [1536], replicated, may hold values from 0.5 to 1.5
- gain_second: float32 [768], replicated, may hold values from 0.5 to 1.5
- grad_output: bfloat16 [8, 16384, 1536], P('fsdp', 'seq'), may hold values from -6 to 6
Outputs:
- grad_input: bfloat16 [8, 16384, 1536], P('fsdp', 'seq')
- grad_gain_first: float32 [1536], replicated
- grad_gain_second: float32 [768], replicated
All inputs are finite; a program needn't handle non-finite values.
Results may differ from a plain program's by a relative error of at most 0.008.
Values may be sent and summed in bfloat16 or wider, within the bound.
No kernel may reach another device: no remote copies, remote signals or barrier semaphores. Data moves between devices by JAX's collectives and lax.ppermute only.
A program may use at most 64 MiB of HBM per device.

v0:
```python
import jax
import jax.numpy as jnp
from jax import lax
from jax.sharding import PartitionSpec as P


def shifted(value, axis, steps):
    count = lax.axis_size(axis)
    initial, last = (max(0, -steps), min(count, count - steps))
    return lax.ppermute(value, axis, [(source, source + steps) for source in range(initial, last)])


def norm_act(values, factor):
    centre = values - jnp.mean(values, axis=-1, keepdims=True)
    spread = jnp.mean(centre * centre, axis=-1, keepdims=True)
    return jax.nn.gelu(centre * lax.rsqrt(spread + 1e-05) * factor)


def far_inputs(values, amount):
    return shifted(values, "seq", amount)


def far_grads(values, amount):
    return shifted(values, "seq", amount)


def three_taps(lagging, hidden_state, leading, w_full):
    mixed_state = jnp.einsum("sbc,ch->sbh", lagging, w_full[0], preferred_element_type=jnp.float32)
    mixed_state = mixed_state + jnp.einsum(
        "sbc,ch->sbh", hidden_state, w_full[1], preferred_element_type=jnp.float32
    )
    return mixed_state + jnp.einsum(
        "sbc,ch->sbh", leading, w_full[2], preferred_element_type=jnp.float32
    )


def block_grads(
    inputs, cotangent, w_full, proj_full, gain_first, gain_second, forward_mix, taps_grad
):
    widened = inputs.astype(jnp.float32)
    hidden_state = norm_act(widened, gain_first).astype(jnp.bfloat16)
    mixed_state = forward_mix(hidden_state).astype(jnp.bfloat16)
    grad_hidden2 = jnp.einsum(
        "sbc,hc->sbh", cotangent, proj_full, preferred_element_type=jnp.float32
    )
    unused, pull_second = jax.vjp(norm_act, mixed_state.astype(jnp.float32), gain_second)
    mixed_gradient, grad_second = pull_second(grad_hidden2)
    mixed_gradient = mixed_gradient.astype(jnp.bfloat16)
    grad_ahead, grad_behind = taps_grad(mixed_gradient)
    hidden_gradient = jnp.einsum(
        "sbh,ch->sbc", grad_ahead, w_full[0], preferred_element_type=jnp.float32
    )
    hidden_gradient = hidden_gradient + jnp.einsum(
        "sbh,ch->sbc", mixed_gradient, w_full[1], preferred_element_type=jnp.float32
    )
    hidden_gradient = hidden_gradient + jnp.einsum(
        "sbh,ch->sbc", grad_behind, w_full[2], preferred_element_type=jnp.float32
    )
    unused2, pull_first = jax.vjp(norm_act, widened, gain_first)
    grad_branch, grad_first = pull_first(hidden_gradient)
    grad_local = (cotangent.astype(jnp.float32) + grad_branch).astype(jnp.bfloat16)
    return (grad_local, grad_first, grad_second)


def body(block_input, dilated_weight, w_project, gain_first, gain_second, grad_output):
    w_full, proj_full = (
        lax.all_gather(dilated_weight, "fsdp", axis=1, tiled=True),
        lax.all_gather(w_project, "fsdp", axis=0, tiled=True),
    )
    reach = lax.axis_size("seq") // 8

    def remote_mix(hidden_state):
        return three_taps(
            far_inputs(hidden_state, reach), hidden_state, far_inputs(hidden_state, -reach), w_full
        )

    def remote_grads(values):
        return (far_grads(values, -reach), far_grads(values, reach))

    grad_input, first_sum, second_sum = block_grads(
        block_input,
        grad_output,
        w_full,
        proj_full,
        gain_first,
        gain_second,
        remote_mix,
        remote_grads,
    )
    totals = lax.psum((first_sum, second_sum), ("seq", "fsdp"))
    return (grad_input, totals[0], totals[1])


def solution(mesh):
    in_specs = (
        P("fsdp", "seq", None),
        P(None, "fsdp", None),
        P("fsdp", None),
        P(),
        P(),
        P("fsdp", "seq", None),
    )
    out_specs = (P("fsdp", "seq", None), P(), P())
    return jax.shard_map(body, mesh=mesh, in_specs=in_specs, out_specs=out_specs, check_vma=False)
```

profile of v0, /device:TPU:1, one launch (start us, length us, event | category | flops | bytes accessed | tf_op | source)
XLA Modules:
  0.0 298.8 jit_solution(9477924018864004862)
XLA Ops:
  7.2 0.0 all-gather.5.cloned.1.call-start
  7.2 0.7 all-gather.5.cloned.1.call-update
  7.9 0.0 all-gather.3.cloned.1.call-start
  8.0 0.7 all-gather.3.cloned.1.call-update
  8.7 0.2 convert_reduce_fusion
  8.9 0.3 fusion.23
  9.2 0.8 fusion.19
  10.0 1.3 collective-permute-start.1
  11.3 6.3 %collective-permute-start = (bf16[2,128,1536]{2,1,0:T(8,128)(2,1)S(1)}, bf16[2,128,1536]{2,1,0:T(8,128)(2,1)S(1)}, u32[]{:S(2)}, u32[]{:S(2)}) collective-permute-start(bf16[2,128,1536]{2,1,0:T(8,128)(2,1)S(1)} %fusion.19), channel_id=1, source_target_pairs={{0,64},{4,68},{8,72},{12,76},{16,80},{20,84},{24,88},{28,92},{32,9... | collective-permute-start | bytes 2359304 | tf_op jit(solution)/shard_map/ppermute | solution.py:10
  17.7 91.2 %all-gather.5.cloned.1.call-done = bf16[3,1536,768]{2,1,0:T(8,128)(2,1)} async-done(((bf16[3,384,768]{2,1,0:T(8,128)(2,1)}), bf16[3,1536,768]{2,1,0:T(8,128)(2,1)}) %all-gather.5.cloned.1.call-update) | async-done | bytes 7077904 | tf_op jit(solution)/shard_map/all_gather | solution.py:67
  108.8 2.4 fusion.5
  111.3 0.0 collective-permute-done.1
  111.3 2.4 fusion.7
  113.7 0.0 copy-start.1
  113.8 0.0 copy-start.3
  113.8 0.0 collective-permute-done
  113.8 2.6 fusion.44
  116.4 0.2 multiply_reduce_fusion.2
  116.6 36.3 %all-gather.3.cloned.1.call-done = bf16[768,1536]{1,0:T(8,128)(2,1)} async-done(((bf16[192,1536]{1,0:T(8,128)(2,1)}), bf16[768,1536]{1,0:T(8,128)(2,1)}) %all-gather.3.cloned.1.call-update) | async-done | bytes 2359312 | tf_op jit(solution)/shard_map/all_gather | solution.py:68
  153.0 3.0 multiply_reduce_fusion.1
  156.0 0.5 multiply_reduce_fusion
  156.4 0.3 add_convert_fusion.1
  156.7 4.4 %collective-permute-start.3 = (bf16[2,128,768]{2,1,0:T(8,128)(2,1)S(1)}, bf16[2,128,768]{2,1,0:T(8,128)(2,1)S(1)}, u32[]{:S(2)}, u32[]{:S(2)}) collective-permute-start(bf16[2,128,768]{2,1,0:T(8,128)(2,1)S(1)} %add_convert_fusion.1), channel_id=1, source_target_pairs={{0,64},{4,68},{8,72},{12,76},{16,80},{20,84},{24,88},{28,92},{32,9... | collective-permute-start | bytes 1179656 | tf_op jit(solution)/shard_map/ppermute | solution.py:10
  161.1 1.3 collective-permute-start.2
  162.4 2.5 fusion.4
  164.9 13.1 %collective-permute-done.3 = bf16[2,128,768]{2,1,0:T(8,128)(2,1)S(1)} collective-permute-done((bf16[2,128,768]{2,1,0:T(8,128)(2,1)S(1)}, bf16[2,128,768]{2,1,0:T(8,128)(2,1)S(1)}, u32[]{:S(2)}, u32[]{:S(2)}) %collective-permute-start.3) | collective-permute-done | bytes 393248 | tf_op jit(solution)/shard_map/ppermute | solution.py:10
  178.0 2.5 fusion.6
  180.5 0.0 collective-permute-done.2
  180.5 3.7 %fusion.24 = (f32[2,128]{1,0:T(2,128)S(1)}, f32[2,128,1536]{2,1,0:T(8,128)S(1)}) fusion(bf16[2,128,1536]{2,1,0:T(8,128)(2,1)S(1)} %copy-done, f32[1536]{0:T(1024)S(1)} %copy-done.2, f32[2,128]{1,0:T(2,128)S(1)} %broadcast_multiply_fusion.1, f32[2,128]{1,0:T(2,128)S(1)} %fusion.42, f32[2,128,1536]{2,1,0:T(8,128)S(1)} %fusion.6, ...), kind=kOutput, calls=%fused_computation.33 | convolution fusion | flops 614989568 | bytes 8266752 | tf_op jit(solution)/shard_map/sbh,ch->sbc/dot_general | solution.py:50
  184.2 0.7 fusion.22
  185.0 1.5 add_convert_fusion
  186.5 105.5 %all-reduce = (f32[1536]{0:T(1024)}, f32[768]{0:T(1024)}) all-reduce(f32[1536]{0:T(1024)S(1)} %get-tuple-element.3, f32[768]{0:T(1024)S(1)} %get-tuple-element.5), channel_id=1, replica_groups=mesh['seq'=128,'fsdp'=4] {'seq','fsdp'}, use_global_device_ids=true, to_apply=%region_9.0 | all-reduce | flops 2304 | bytes 18432 | tf_op jit(solution)/shard_map/psum | solution.py:90
  (14 shorter events, 0.1 us)
Async XLA Ops:
  7.2 1.5 copy-start
  7.2 2.1 copy-start.2
  7.2 101.7 %all-gather.5.cloned.1.call-start = ((), (), s32[]{:S(2)}) async-start(), calls=%async_computation.1 | async-start | bytes 8847360 | tf_op jit(solution)/shard_map/all_gather | solution.py:67
  7.9 145.0 %all-gather.3.cloned.1.call-start = ((), (), s32[]{:S(2)}) async-start(), calls=%async_computation | async-start | bytes 2949120 | tf_op jit(solution)/shard_map/all_gather | solution.py:68
  10.0 101.3 %collective-permute-start.1 = (bf16[2,128,1536]{2,1,0:T(8,128)(2,1)S(1)}, bf16[2,128,1536]{2,1,0:T(8,128)(2,1)S(1)}, u32[]{:S(2)}, u32[]{:S(2)}) collective-permute-start(bf16[2,128,1536]{2,1,0:T(8,128)(2,1)S(1)} %fusion.19), channel_id=1, source_target_pairs={{64,0},{68,4},{72,8},{76,12},{80,16},{84,20},{88,24},{92,28},{96,3... | collective-permute-start | bytes 2359304 | tf_op jit(solution)/shard_map/ppermute | solution.py:10
  11.3 102.4 %collective-permute-start = (bf16[2,128,1536]{2,1,0:T(8,128)(2,1)S(1)}, bf16[2,128,1536]{2,1,0:T(8,128)(2,1)S(1)}, u32[]{:S(2)}, u32[]{:S(2)}) collective-permute-start(bf16[2,128,1536]{2,1,0:T(8,128)(2,1)S(1)} %fusion.19), channel_id=1, source_target_pairs={{0,64},{4,68},{8,72},{12,76},{16,80},{20,84},{24,88},{28,92},{32,9... | collective-permute-start | bytes 2359304 | tf_op jit(solution)/shard_map/ppermute | solution.py:10
  113.7 39.2 %copy-start.1 = (bf16[2,128,1536]{2,1,0:T(8,128)(2,1)S(1)}, bf16[2,128,1536]{2,1,0:T(8,128)(2,1)}, u32[]{:S(2)}) copy-start(bf16[2,128,1536]{2,1,0:T(8,128)(2,1)} %param.11) | copy-start | bytes 2359300
  113.8 39.2 %copy-start.3 = (f32[768]{0:T(1024)S(1)}, f32[768]{0:T(1024)}, u32[]{:S(2)}) copy-start(f32[768]{0:T(1024)} %param.10) | copy-start | bytes 9220
  156.7 21.3 %collective-permute-start.3 = (bf16[2,128,768]{2,1,0:T(8,128)(2,1)S(1)}, bf16[2,128,768]{2,1,0:T(8,128)(2,1)S(1)}, u32[]{:S(2)}, u32[]{:S(2)}) collective-permute-start(bf16[2,128,768]{2,1,0:T(8,128)(2,1)S(1)} %add_convert_fusion.1), channel_id=1, source_target_pairs={{0,64},{4,68},{8,72},{12,76},{16,80},{20,84},{24,88},{28,92},{32,9... | collective-permute-start | bytes 1179656 | tf_op jit(solution)/shard_map/ppermute | solution.py:10
  161.1 19.4 %collective-permute-start.2 = (bf16[2,128,768]{2,1,0:T(8,128)(2,1)S(1)}, bf16[2,128,768]{2,1,0:T(8,128)(2,1)S(1)}, u32[]{:S(2)}, u32[]{:S(2)}) collective-permute-start(bf16[2,128,768]{2,1,0:T(8,128)(2,1)S(1)} %add_convert_fusion.1), channel_id=1, source_target_pairs={{64,0},{68,4},{72,8},{76,12},{80,16},{84,20},{88,24},{92,28},{96,3... | collective-permute-start | bytes 1179656 | tf_op jit(solution)/shard_map/ppermute | solution.py:10
Sparse Core Ops, SparseCore 0:
  10.1 98.6 all-gather.4
  110.9 41.9 all-gather.2
where the time goes:
time: 299 us
  waiting for transfers between devices  142 us (47%)
  blocking collectives  106 us (35%)
  matrix products  19.1 us (6%)
  between operations  14.2 us (5%)
  starting transfers between devices  13.4 us (4%)
  other arithmetic  4.61 us (2%)
    psum x1, blocking collectives, body(): totals = lax.psum((first_sum, second_sum), ('seq', 'fsdp'))  106 us
    all_gather x1, waiting for transfers between devices, body(): lax.all_gather(dilated_weight, 'fsdp', axis=1, tiled=True)  91.2 us
    all_gather x1, waiting for transfers between devices, body(): lax.all_gather(w_project, 'fsdp', axis=0, tiled=True)  36.3 us
    ppermute x4, starting transfers between devices, shifted(): lax.ppermute(value, axis, [(source, source + steps) for source in range(i...  13.3 us
    ppermute x4, waiting for transfers between devices, shifted(): lax.ppermute(value, axis, [(source, source + steps) for source in range(i...  13.1 us
  transfers between devices with their start and end apart: 6, of which 3 were waited for; matrix products, arithmetic and copies ran while one was open for 5% of the time, Pallas kernels for 0%

commit v1 on v0

--- a/solution.py
+++ b/solution.py
@@ -2,6 +2,12 @@
 import jax.numpy as jnp
 from jax import lax
 from jax.sharding import PartitionSpec as P
+
+
+def tiles_touch(field_in):
+    for src_i in ("seq", "fsdp"):
+        field_in = lax.psum(field_in, src_i)
+    return field_in
 
 
 def shifted(value, axis, steps):
@@ -87,7 +93,7 @@
         remote_mix,
         remote_grads,
     )
-    totals = lax.psum((first_sum, second_sum), ("seq", "fsdp"))
+    totals = tiles_touch((first_sum, second_sum))
     return (grad_input, totals[0], totals[1])
 
 

time: 299 us -> 908 us (3.04)
  blocking collectives: 106 us -> 715 us
    psum x1 -> x2, blocking collectives: 106 us -> 715 us  [tiles_touch(): field_in = lax.psum(field_in, src_i)]
  transfers between devices with their start and end apart: 6 -> 6, of which waited for: 3 -> 3; matrix products, arithmetic and copies ran while one was open for 5% -> 2% of each run, Pallas kernels for 0% -> 0%
where the time goes in v1:
time: 908 us
  blocking collectives  715 us (79%)
  waiting for transfers between devices  142 us (16%)
  matrix products  19.1 us (2%)
  between operations  14.2 us (2%)
  starting transfers between devices  13.4 us (1%)
    psum x2, blocking collectives, tiles_touch(): field_in = lax.psum(field_in, src_i)  715 us
    all_gather x1, waiting for transfers between devices, body(): lax.all_gather(dilated_weight, 'fsdp', axis=1, tiled=True)  91.2 us
    all_gather x1, waiting for transfers between devices, body(): lax.all_gather(w_project, 'fsdp', axis=0, tiled=True)  36.3 us
  transfers between devices with their start and end apart: 6, of which 3 were waited for; matrix products, arithmetic and copies ran while one was open for 2% of the time, Pallas kernels for 0%

profile of v1, /device:TPU:1, one launch (start us, length us, event | category | flops | bytes accessed | tf_op | source)
XLA Modules:
  0.0 907.9 jit_solution(16876836173069426962)
XLA Ops:
  7.2 0.0 all-gather.5.cloned.1.call-start
  7.2 0.7 all-gather.5.cloned.1.call-update
  7.9 0.0 all-gather.3.cloned.1.call-start
  8.0 0.7 all-gather.3.cloned.1.call-update
  8.7 0.2 convert_reduce_fusion
  8.9 0.3 fusion.23
  9.2 0.8 fusion.19
  10.0 1.3 collective-permute-start.1
  11.3 6.3 collective-permute-start
  17.7 91.2 %all-gather.5.cloned.1.call-done = bf16[3,1536,768]{2,1,0:T(8,128)(2,1)} async-done(((bf16[3,384,768]{2,1,0:T(8,128)(2,1)}), bf16[3,1536,768]{2,1,0:T(8,128)(2,1)}) %all-gather.5.cloned.1.call-update) | async-done | bytes 7077904 | tf_op jit(solution)/shard_map/all_gather | solution.py:73
  108.8 2.4 fusion.5
  111.3 2.4 fusion.7
  113.7 0.0 copy-start.1
  113.8 0.0 copy-start.3
  113.8 0.0 collective-permute-done
  113.8 2.6 fusion.44
  116.4 0.2 multiply_reduce_fusion.2
  116.6 36.3 %all-gather.3.cloned.1.call-done = bf16[768,1536]{1,0:T(8,128)(2,1)} async-done(((bf16[192,1536]{1,0:T(8,128)(2,1)}), bf16[768,1536]{1,0:T(8,128)(2,1)}) %all-gather.3.cloned.1.call-update) | async-done | bytes 2359312 | tf_op jit(solution)/shard_map/all_gather | solution.py:74
  153.0 3.0 multiply_reduce_fusion.1
  156.0 0.5 multiply_reduce_fusion
  156.4 0.3 add_convert_fusion.1
  156.7 4.4 collective-permute-start.3
  161.1 1.3 collective-permute-start.2
  162.4 2.5 fusion.4
  164.9 13.1 %collective-permute-done.3 = bf16[2,128,768]{2,1,0:T(8,128)(2,1)S(1)} collective-permute-done((bf16[2,128,768]{2,1,0:T(8,128)(2,1)S(1)}, bf16[2,128,768]{2,1,0:T(8,128)(2,1)S(1)}, u32[]{:S(2)}, u32[]{:S(2)}) %collective-permute-start.3) | collective-permute-done | bytes 393248 | tf_op jit(solution)/shard_map/ppermute | solution.py:16
  178.0 2.5 fusion.6
  180.5 0.0 collective-permute-done.2
  180.5 3.7 fusion.24
  184.2 0.7 fusion.22
  185.0 1.5 add_convert_fusion
  186.5 594.7 %all-reduce = (f32[1536]{0:T(1024)S(1)}, f32[768]{0:T(1024)S(1)}) all-reduce(f32[1536]{0:T(1024)S(1)} %get-tuple-element.3, f32[768]{0:T(1024)S(1)} %get-tuple-element.5), channel_id=1, replica_groups=mesh['seq'=128,'fsdp'=4] {'seq'}, use_global_device_ids=true, to_apply=%region_9.0 | all-reduce | flops 2304 | bytes 18432 | tf_op jit(solution)/shard_map/psum | solution.py:9
  781.2 119.8 %all-reduce.1 = (f32[1536]{0:T(1024)}, f32[768]{0:T(1024)}) all-reduce(f32[1536]{0:T(1024)S(1)} %get-tuple-element.7, f32[768]{0:T(1024)S(1)} %get-tuple-element.8), channel_id=1, replica_groups=mesh['seq'=128,'fsdp'=4] {'fsdp'}, use_global_device_ids=true, to_apply=%region_10.0 | all-reduce | flops 2304 | bytes 18432 | tf_op jit(solution)/shard_map/psum | solution.py:9
  (15 shorter events, 0.1 us)
Async XLA Ops:
  7.2 1.5 copy-start
  7.2 2.1 copy-start.2
  7.2 101.7 %all-gather.5.cloned.1.call-start = ((), (), s32[]{:S(2)}) async-start(), calls=%async_computation.1 | async-start | bytes 8847360 | tf_op jit(solution)/shard_map/all_gather | solution.py:73
  7.9 145.0 %all-gather.3.cloned.1.call-start = ((), (), s32[]{:S(2)}) async-start(), calls=%async_computation | async-start | bytes 2949120 | tf_op jit(solution)/shard_map/all_gather | solution.py:74
  10.0 101.3 %collective-permute-start.1 = (bf16[2,128,1536]{2,1,0:T(8,128)(2,1)S(1)}, bf16[2,128,1536]{2,1,0:T(8,128)(2,1)S(1)}, u32[]{:S(2)}, u32[]{:S(2)}) collective-permute-start(bf16[2,128,1536]{2,1,0:T(8,128)(2,1)S(1)} %fusion.19), channel_id=1, source_target_pairs={{64,0},{68,4},{72,8},{76,12},{80,16},{84,20},{88,24},{92,28},{96,3... | collective-permute-start | bytes 2359304 | tf_op jit(solution)/shard_map/ppermute | solution.py:16
  11.3 102.4 %collective-permute-start = (bf16[2,128,1536]{2,1,0:T(8,128)(2,1)S(1)}, bf16[2,128,1536]{2,1,0:T(8,128)(2,1)S(1)}, u32[]{:S(2)}, u32[]{:S(2)}) collective-permute-start(bf16[2,128,1536]{2,1,0:T(8,128)(2,1)S(1)} %fusion.19), channel_id=1, source_target_pairs={{0,64},{4,68},{8,72},{12,76},{16,80},{20,84},{24,88},{28,92},{32,9... | collective-permute-start | bytes 2359304 | tf_op jit(solution)/shard_map/ppermute | solution.py:16
  113.7 39.2 %copy-start.1 = (bf16[2,128,1536]{2,1,0:T(8,128)(2,1)S(1)}, bf16[2,128,1536]{2,1,0:T(8,128)(2,1)}, u32[]{:S(2)}) copy-start(bf16[2,128,1536]{2,1,0:T(8,128)(2,1)} %param.11) | copy-start | bytes 2359300
  113.8 39.2 %copy-start.3 = (f32[768]{0:T(1024)S(1)}, f32[768]{0:T(1024)}, u32[]{:S(2)}) copy-start(f32[768]{0:T(1024)} %param.10) | copy-start | bytes 9220
  156.7 21.3 %collective-permute-start.3 = (bf16[2,128,768]{2,1,0:T(8,128)(2,1)S(1)}, bf16[2,128,768]{2,1,0:T(8,128)(2,1)S(1)}, u32[]{:S(2)}, u32[]{:S(2)}) collective-permute-start(bf16[2,128,768]{2,1,0:T(8,128)(2,1)S(1)} %add_convert_fusion.1), channel_id=1, source_target_pairs={{0,64},{4,68},{8,72},{12,76},{16,80},{20,84},{24,88},{28,92},{32,9... | collective-permute-start | bytes 1179656 | tf_op jit(solution)/shard_map/ppermute | solution.py:16
  161.1 19.4 %collective-permute-start.2 = (bf16[2,128,768]{2,1,0:T(8,128)(2,1)S(1)}, bf16[2,128,768]{2,1,0:T(8,128)(2,1)S(1)}, u32[]{:S(2)}, u32[]{:S(2)}) collective-permute-start(bf16[2,128,768]{2,1,0:T(8,128)(2,1)S(1)} %add_convert_fusion.1), channel_id=1, source_target_pairs={{64,0},{68,4},{72,8},{76,12},{80,16},{84,20},{88,24},{92,28},{96,3... | collective-permute-start | bytes 1179656 | tf_op jit(solution)/shard_map/ppermute | solution.py:16
Sparse Core Ops, SparseCore 0:
  10.1 98.6 all-gather.4
  110.9 41.9 all-gather.2
